TPU v7x, 32 devices: a whole 2x2x4 slice. The times are simulated.
32 devices in a mesh: context: 4 (over z), tensor: 2 (over core), dp: 4 (over y, x).
Axes of the slice: x: 2, y: 2, z: 4, core: 2. Of those that a mesh axis runs over, the one named last changes fastest.
Arguments:
- queries: bfloat16 [4, 3072, 2048], P('dp', 'context', 'tensor'), may hold values from -1.75 to 1.75
- keys_in: bfloat16 [4, 3072, 2048], P('dp', 'context', 'tensor'), may hold values from -1.75 to 1.75
- values: bfloat16 [4, 3072, 2048], P('dp', 'context', 'tensor'), may hold values from -48 to 48
- norm_gain: float32 [2048], P('tensor'), may hold values from 0.25 to 1.75
- segment_ids: int32 [4, 48], P('dp', 'context'), may hold values from 0 to 5, never falling along the last dimension, each value on 1 to 24 neighbouring positions
- grad_out: bfloat16 [4, 3072, 2048], P('dp', 'context', 'tensor'), may hold values from -8 to 8
Outputs:
- normed_out: bfloat16 [4, 3072, 2048], P('dp', 'context', 'tensor')
- grad_queries: bfloat16 [4, 3072, 2048], P('dp', 'context', 'tensor')
- grad_keys: bfloat16 [4, 3072, 2048], P('dp', 'context', 'tensor')
- grad_values: bfloat16 [4, 3072, 2048], P('dp', 'context', 'tensor')
- grad_gain: float32 [2048], P('tensor')
Inputs may be any that keep to these rules, and one draw needn't show every extreme that they name: `segment_ids`: along each sequence the ids never fall; each id is one document.
All inputs are finite; a program needn't handle non-finite values.
Results may differ from a plain program's by a relative error of at most 0.0057.
Values sent between devices are 32-bit elements; how exact they have to be, the bound alone decides.
A program may use at most 128 MiB of HBM per device.

v0:
```python
import jax
import jax.numpy as jnp
from jax import lax
from jax.sharding import PartitionSpec as P

HD = 128
BLK = 256
SEGB = 64
WIDTH = 2048


def shifted(block, axis, distance):
    devices = range(lax.axis_size(axis))
    route = [(i - distance, i) for i in devices if i - distance in devices]
    return lax.ppermute(block, axis, route)


def prefix(value, axis, combine, identity):
    size, place = (lax.axis_size(axis), lax.axis_index(axis))
    everything = jax.tree.map(lambda part: lax.all_gather(part, axis), value)
    start = jax.tree.map(
        lambda part, zero: jnp.broadcast_to(jnp.asarray(zero, part.dtype), part.shape),
        value,
        identity,
    )

    def step(k, before):
        at = size - 1 - k
        reached = at > place
        new = combine(before, jax.tree.map(lambda part: part[at], everything))
        return jax.tree.map(lambda a, b: jnp.where(reached, a, b), new, before)

    return lax.fori_loop(0, size, step, start)


def join_forward(earlier, later):
    early_state, early_segs = earlier
    late_state, late_segs = later
    matches = jnp.logical_or(
        jnp.logical_and(early_segs[1] == late_segs[0], late_segs[0] == late_segs[1]),
        late_segs[0] == 0.0,
    )
    joined = late_state + jnp.where(matches, early_state, 0.0)
    first_seg = jnp.where(early_segs[0] == 0.0, late_segs[0], early_segs[0])
    last_seg = jnp.where(late_segs[1] == 0.0, early_segs[1], late_segs[1])
    return (joined, jnp.stack([first_seg, last_seg]))


def join_backward(earlier, later):
    high_state, high_segs = earlier
    low_state, low_segs = later
    matches = jnp.logical_or(
        jnp.logical_and(high_segs[0] == low_segs[1], low_segs[0] == low_segs[1]), low_segs[0] == 0.0
    )
    joined = low_state + jnp.where(matches, high_state, 0.0)
    first_seg = jnp.where(low_segs[0] == 0.0, high_segs[0], low_segs[0])
    last_seg = jnp.where(high_segs[1] == 0.0, low_segs[1], high_segs[1])
    return (joined, jnp.stack([first_seg, last_seg]))


def block_mask(seg_block):
    length = seg_block.shape[0]
    row_index = lax.broadcasted_iota(jnp.int32, (length, length), 0)
    col_index = lax.broadcasted_iota(jnp.int32, (length, length), 1)
    return jnp.logical_and(row_index >= col_index, seg_block[:, None] == seg_block[None, :])


def forward_block(carried, block_in):
    kv_state, seg_prev = carried
    q_block, k_block, v_block, seg_block = block_in
    visible = block_mask(seg_block)
    scores = jnp.einsum("thd,shd->hts", q_block, k_block, preferred_element_type=jnp.float32)
    weights = jnp.where(visible[None], scores, 0.0).astype(jnp.bfloat16)
    intra = jnp.einsum("hts,she->the", weights, v_block, preferred_element_type=jnp.float32)
    state_bf = kv_state.astype(jnp.bfloat16)
    inter = jnp.einsum("thd,hde->the", q_block, state_bf, preferred_element_type=jnp.float32)
    matches = (seg_block == seg_prev)[:, None, None]
    attended = intra + jnp.where(matches, inter, 0.0)
    last_seg = seg_block[-1]
    in_last = (seg_block == last_seg)[:, None, None]
    added = jnp.einsum(
        "thd,the->hde",
        jnp.where(in_last, k_block, jnp.zeros_like(k_block)),
        v_block,
        preferred_element_type=jnp.float32,
    )
    new_state = jnp.where(seg_prev == last_seg, kv_state, 0.0) + added
    return ((new_state, last_seg), (attended, weights, state_bf, seg_prev))


def backward_block(grad_state, block_in):
    q_block, k_block, v_block, seg_block, grad_block, weights, state_bf, seg_prev = block_in
    visible = block_mask(seg_block)
    grad_scores = jnp.einsum(
        "the,she->hts", grad_block, v_block, preferred_element_type=jnp.float32
    )
    grad_weights = jnp.where(visible[None], grad_scores, 0.0).astype(jnp.bfloat16)
    grad_bf = grad_state.astype(jnp.bfloat16)
    before = (seg_block == seg_prev)[:, None, None]
    after = (seg_block == seg_block[-1])[:, None, None]
    grad_q = jnp.einsum("hts,shd->thd", grad_weights, k_block, preferred_element_type=jnp.float32)
    grad_q = grad_q + jnp.where(
        before,
        jnp.einsum("the,hde->thd", grad_block, state_bf, preferred_element_type=jnp.float32),
        0.0,
    )
    grad_k = jnp.einsum("hts,thd->shd", grad_weights, q_block, preferred_element_type=jnp.float32)
    grad_k = grad_k + jnp.where(
        after, jnp.einsum("she,hde->shd", v_block, grad_bf, preferred_element_type=jnp.float32), 0.0
    )
    grad_v = jnp.einsum("hts,the->she", weights, grad_block, preferred_element_type=jnp.float32)
    grad_v = grad_v + jnp.where(
        after, jnp.einsum("shd,hde->she", k_block, grad_bf, preferred_element_type=jnp.float32), 0.0
    )
    added = jnp.einsum(
        "thd,the->hde",
        jnp.where(before, q_block, jnp.zeros_like(q_block)),
        grad_block,
        preferred_element_type=jnp.float32,
    )
    new_grad = jnp.where(seg_prev == seg_block[-1], grad_state, 0.0) + added
    return (
        new_grad,
        (grad_q.astype(jnp.bfloat16), grad_k.astype(jnp.bfloat16), grad_v.astype(jnp.bfloat16)),
    )


def body(queries, keys_in, values, norm_gain, segment_ids, grad_out):
    tok_count = queries.shape[1]
    local_width = queries.shape[2]
    head_count = local_width // HD
    block_count = tok_count // BLK
    seg_tok = jnp.repeat(segment_ids[0], SEGB)
    seg_blocks = seg_tok.reshape(block_count, BLK)
    flat_q = queries[0].reshape(tok_count, head_count, HD)
    flat_k = keys_in[0].reshape(tok_count, head_count, HD)
    flat_v = values[0].reshape(tok_count, head_count, HD)
    first_seg = seg_tok[0]
    last_seg = seg_tok[-1]
    own_segs = jnp.stack([first_seg + 1, last_seg + 1]).astype(jnp.float32)
    in_last = (seg_tok == last_seg)[:, None, None]
    own_kv = jnp.einsum(
        "thd,the->hde",
        jnp.where(in_last, flat_k, jnp.zeros_like(flat_k)),
        flat_v,
        preferred_element_type=jnp.float32,
    )
    empty = (jnp.zeros_like(own_kv), jnp.zeros((2,), jnp.float32))

    def relay_step(step_index, incoming):
        return shifted(join_forward(incoming, (own_kv, own_segs)), "context", 1)

    arrived = lax.fori_loop(0, lax.axis_size("context") - 1, relay_step, empty)
    state_in = jnp.where(arrived[1][1] == own_segs[0], arrived[0], 0.0)
    block_q = flat_q.reshape(block_count, BLK, head_count, HD)
    block_k = flat_k.reshape(block_count, BLK, head_count, HD)
    block_v = flat_v.reshape(block_count, BLK, head_count, HD)
    final, stored = lax.scan(
        forward_block, (state_in, first_seg), (block_q, block_k, block_v, seg_blocks)
    )
    attended_blocks, weights_all, state_all, prev_all = stored
    attended = attended_blocks.reshape(tok_count, local_width)
    cotangent = grad_out[0].astype(jnp.float32)
    gained = cotangent * norm_gain
    squares, inner = lax.psum(
        (jnp.sum(attended * attended, axis=1), jnp.sum(gained * attended, axis=1)), "tensor"
    )
    radius = jnp.sqrt(squares / WIDTH + 1e-06)
    normed = attended / radius[:, None]
    normed_out = (normed * norm_gain).astype(jnp.bfloat16)
    grad_gain = lax.psum(jnp.sum(cotangent * normed, axis=0), ("context", "dp"))
    grad_att = (
        (gained - attended * (inner / (WIDTH * radius * radius))[:, None]) / radius[:, None]
    ).astype(jnp.bfloat16)
    flat_da = grad_att.reshape(tok_count, head_count, HD)
    in_first = (seg_tok == first_seg)[:, None, None]
    own_grad = jnp.einsum(
        "thd,the->hde",
        jnp.where(in_first, flat_q, jnp.zeros_like(flat_q)),
        flat_da,
        preferred_element_type=jnp.float32,
    )
    behind = prefix((own_grad, own_segs), "context", join_backward, empty)
    grad_in = jnp.where(behind[1][0] == own_segs[1], behind[0], 0.0)
    block_da = flat_da.reshape(block_count, BLK, head_count, HD)
    leftover, grads = lax.scan(
        backward_block,
        grad_in,
        (block_q, block_k, block_v, seg_blocks, block_da, weights_all, state_all, prev_all),
        reverse=True,
    )
    grad_queries = grads[0].reshape(1, tok_count, local_width)
    grad_keys = grads[1].reshape(1, tok_count, local_width)
    grad_values = grads[2].reshape(1, tok_count, local_width)
    return (
        normed_out.reshape(1, tok_count, local_width),
        grad_queries,
        grad_keys,
        grad_values,
        grad_gain,
    )


def solution(mesh):
    in_specs = (
        P("dp", "context", "tensor"),
        P("dp", "context", "tensor"),
        P("dp", "context", "tensor"),
        P("tensor"),
        P("dp", "context"),
        P("dp", "context", "tensor"),
    )
    out_specs = (
        P("dp", "context", "tensor"),
        P("dp", "context", "tensor"),
        P("dp", "context", "tensor"),
        P("dp", "context", "tensor"),
        P("tensor"),
    )
    return jax.shard_map(body, mesh=mesh, in_specs=in_specs, out_specs=out_specs, check_vma=False)
```

profile of v0, /device:TPU:0, one launch (start us, length us, event | category | flops | bytes accessed | tf_op | source)
XLA Modules:
  0.0 330.4 jit_solution(14289737301600793897)
XLA Ops:
  20.1 50.7 %while.71 = (s32[]{:T(128)}, f32[8,128,128]{2,1,0:T(8,128)S(1)}, f32[2]{0:T(128)S(1)}, f32[2]{0:T(128)S(1)}, pred[]{:T(512)}, /*index=5*/pred[]{:T(512)}, f32[8,...) while((s32[]{:T(128)}, f32[8,128,128]{2,1,0:T(8,128)S(1)}, f32[2]{0:T(128)S(1)}, f32[2]{0:T(128)S(1)}, ...), condition=%wide.region_1.2_spmd, body=%wide.region_0.1_spmd.sunk | while | flops 262154 | bytes 3670328 | solution.py:153
  22.2 5.0 %collective-permute-start = (f32[8,128,128]{2,1,0:T(8,128)S(1)}, f32[8,128,128]{2,1,0:T(8,128)S(1)}, u32[]{:S(2)}, u32[]{:S(2)}) collective-permute-start(f32[8,128,128]{2,1,0:T(8,128)S(1)} %select_add_fusion.2), channel_id=1, source_target_pairs={{0,8},{8,16},{16,24},{1,9},{9,17},{17,25},{2,10},{10,18},{18,26},{... | collective-permute-start | bytes 1572872 | tf_op jit(solution)/shard_map/while/body/eval_jaxpr/ppermute | solution.py:15
  30.5 3.4 %collective-permute-start.1 = (f32[2]{0:T(128)S(1)}, f32[2]{0:T(128)S(1)}, u32[]{:S(2)}, u32[]{:S(2)}) collective-permute-start(f32[2]{0:T(128)S(1)} %pad_maximum_fusion.2), channel_id=1, source_target_pairs={{0,8},{8,16},{16,24},{1,9},{9,17},{17,25},{2,10},{10,18},{18,26},{... | collective-permute-start | bytes 32 | tf_op jit(solution)/shard_map/while/body/eval_jaxpr/ppermute | solution.py:15
  33.9 4.4 %collective-permute-done.1 = f32[2]{0:T(128)S(1)} collective-permute-done((f32[2]{0:T(128)S(1)}, f32[2]{0:T(128)S(1)}, u32[]{:S(2)}, u32[]{:S(2)}) %collective-permute-start.1) | collective-permute-done | bytes 40 | tf_op jit(solution)/shard_map/while/body/eval_jaxpr/ppermute | solution.py:15
  40.4 4.4 %collective-permute-start = (f32[8,128,128]{2,1,0:T(8,128)S(1)}, f32[8,128,128]{2,1,0:T(8,128)S(1)}, u32[]{:S(2)}, u32[]{:S(2)}) collective-permute-start(f32[8,128,128]{2,1,0:T(8,128)S(1)} %select_add_fusion.2), channel_id=1, source_target_pairs={{0,8},{8,16},{16,24},{1,9},{9,17},{17,25},{2,10},{10,18},{18,26},{... | collective-permute-start | bytes 1572872 | tf_op jit(solution)/shard_map/while/body/eval_jaxpr/ppermute | solution.py:15
  48.2 3.4 %collective-permute-start.1 = (f32[2]{0:T(128)S(1)}, f32[2]{0:T(128)S(1)}, u32[]{:S(2)}, u32[]{:S(2)}) collective-permute-start(f32[2]{0:T(128)S(1)} %pad_maximum_fusion.2), channel_id=1, source_target_pairs={{0,8},{8,16},{16,24},{1,9},{9,17},{17,25},{2,10},{10,18},{18,26},{... | collective-permute-start | bytes 32 | tf_op jit(solution)/shard_map/while/body/eval_jaxpr/ppermute | solution.py:15
  51.6 3.5 %collective-permute-done.1 = f32[2]{0:T(128)S(1)} collective-permute-done((f32[2]{0:T(128)S(1)}, f32[2]{0:T(128)S(1)}, u32[]{:S(2)}, u32[]{:S(2)}) %collective-permute-start.1) | collective-permute-done | bytes 40 | tf_op jit(solution)/shard_map/while/body/eval_jaxpr/ppermute | solution.py:15
  57.2 4.4 %collective-permute-start = (f32[8,128,128]{2,1,0:T(8,128)S(1)}, f32[8,128,128]{2,1,0:T(8,128)S(1)}, u32[]{:S(2)}, u32[]{:S(2)}) collective-permute-start(f32[8,128,128]{2,1,0:T(8,128)S(1)} %select_add_fusion.2), channel_id=1, source_target_pairs={{0,8},{8,16},{16,24},{1,9},{9,17},{17,25},{2,10},{10,18},{18,26},{... | collective-permute-start | bytes 1572872 | tf_op jit(solution)/shard_map/while/body/eval_jaxpr/ppermute | solution.py:15
  64.9 3.4 %collective-permute-start.1 = (f32[2]{0:T(128)S(1)}, f32[2]{0:T(128)S(1)}, u32[]{:S(2)}, u32[]{:S(2)}) collective-permute-start(f32[2]{0:T(128)S(1)} %pad_maximum_fusion.2), channel_id=1, source_target_pairs={{0,8},{8,16},{16,24},{1,9},{9,17},{17,25},{2,10},{10,18},{18,26},{... | collective-permute-start | bytes 32 | tf_op jit(solution)/shard_map/while/body/eval_jaxpr/ppermute | solution.py:15
  74.2 3.1 copy.106
  80.4 31.8 %while.72 = (s32[]{:T(128)}, f32[8,128,128]{2,1,0:T(8,128)S(1)}, s32[]{:T(128)}, f32[3,256,8,128]{1,3,2,0:T(8,128)}, bf16[3,8,256,256]{3,2,1,0:T(8,128)(2,1)}, /...) while((s32[]{:T(128)}, f32[8,128,128]{2,1,0:T(8,128)S(1)}, ...), condition=%wide.region_3.4_spmd, body=%wide.region_2.3_spmd.sunk | while | flops 405209600 | bytes 18224672 | solution.py:158
  113.4 2.5 copy.70
  118.1 2.6 copy.93
  128.9 4.9 %fusion.54 = bf16[768,8,128]{2,1,0:T(8,128)(2,1)S(1)} fusion(f32[96,8,8,128]{3,2,1,0:T(8,128)} %copy-done.6, f32[3,256,8,128]{3,2,1,0:T(8,128)S(1)} %copy.70, f32[768]{0:T(1024)S(1)} %get-tuple-element.728, f32[768]{0:T(1024)S(1)} %get-tuple-element.727, f32[8,128]{1,0:T(8,128)S(1)} %bitcast.320), kind=kLoop, calls=%fused_computation.98 | loop fusion | flops 3932160 | bytes 7874560 | tf_op jit(solution)/shard_map/convert_element_type | solution.py:174
  135.3 12.0 %all-gather.1 = f32[4,1,2]{2,1,0:T(1,128)S(1)} all-gather(f32[1,1,2]{2,1,0:T(1,128)S(1)} %fusion.66), channel_id=1, replica_groups=mesh['context'=4,'tensor'=2,'dp'=4] {'context'}, dimensions={0}, use_global_device_ids=true | all-gather | bytes 40 | tf_op jit(solution)/shard_map/all_gather | solution.py:20
  152.2 39.9 %psum.23 = f32[1024]{0:T(1024)} all-reduce(f32[1024]{0:T(1024)S(1)} %fusion.51), channel_id=1, replica_groups=mesh['context'=4,'tensor'=2,'dp'=4] {'context','dp'}, use_global_device_ids=true, to_apply=%region_13.14 | all-reduce | flops 1024 | bytes 8192 | tf_op jit(solution)/shard_map/psum | solution.py:171
  192.2 3.7 %multiply_convert_fusion = bf16[1,768,1024]{2,1,0:T(8,128)(2,1)} fusion(f32[1,768,1024]{2,1,0:T(8,128)} %reshape.302, f32[1024]{0:T(1024)S(1)} %copy-done.15, f32[768]{0:T(1024)S(1)} %get-tuple-element.728), kind=kLoop, calls=%fused_computation.102 | loop fusion | flops 2359296 | bytes 4725760 | tf_op jit(solution)/shard_map/convert_element_type | solution.py:170
  195.9 2.9 divide_convert_fusion
  198.8 39.5 %while.74 = (s32[]{:T(128)}, f32[8,128,128]{2,1,0:T(8,128)}, f32[2]{0:T(128)S(1)}, s32[]{:T(128)}, f32[4,8,128,128]{3,2,1,0:T(8,128)}, /*index=5*/f32[4,2]{0,1:T...) while((s32[]{:T(128)}, f32[8,128,128]{2,1,0:T(8,128)}, ...), condition=%wide.region_9.10_spmd.clone, body=%wide.region_8.9_spmd.clone.sunk | while | flops 524312 | bytes 1573215 | solution.py:33
  244.1 71.5 %while.73 = (s32[]{:T(128)}, f32[8,128,128]{2,1,0:T(8,128)S(1)}, bf16[3,256,8,128]{3,2,1,0:T(8,128)(2,1)}, bf16[3,256,8,128]{3,2,1,0:T(8,128)(2,1)}, bf16[3,256,...) while((s32[]{:T(128)}, f32[8,128,128]{2,1,0:T(8,128)S(1)}, ...), condition=%wide.region_11.12_spmd, body=%wide.region_10.11_spmd.sunk | while | flops 809697792 | bytes 39720800 | solution.py:186
  245.3 2.5 select_convert_fusion.3
  269.2 2.5 select_convert_fusion.3
  293.0 2.5 select_convert_fusion.3
  315.7 3.8 %reshape.304 = bf16[1,768,1024]{2,1,0:T(8,128)(2,1)} reshape(bf16[3,256,8,128]{3,2,1,0:T(8,128)(2,1)} %get-tuple-element.544) | data formatting | bytes 3145728 | tf_op jit(solution)/shard_map/reshape | solution.py:192
  (240 shorter events, 147.2 us)
Async XLA Ops:
  7.2 191.7 %all-gather.4.cloned.1.call-start = ((), (), s32[]{:S(2)}) async-start(), calls=%async_computation | async-start | bytes 2621440 | tf_op jit(solution)/shard_map/all_gather | solution.py:20
  14.4 2.0 copy-start.8
  16.4 1.7 copy-start.10
  20.1 53.1 %copy-start.16 = (s32[1,12]{1,0:T(1,128)S(1)}, s32[1,12]{1,0:T(1,128)}, u32[]{:S(2)}) copy-start(s32[1,12]{1,0:T(1,128)} %param.18) | copy-start | bytes 148
  22.2 16.1 %collective-permute-start = (f32[8,128,128]{2,1,0:T(8,128)S(1)}, f32[8,128,128]{2,1,0:T(8,128)S(1)}, u32[]{:S(2)}, u32[]{:S(2)}) collective-permute-start(f32[8,128,128]{2,1,0:T(8,128)S(1)} %select_add_fusion.2), channel_id=1, source_target_pairs={{0,8},{8,16},{16,24},{1,9},{9,17},{17,25},{2,10},{10,18},{18,26},{... | collective-permute-start | bytes 1572872 | tf_op jit(solution)/shard_map/while/body/eval_jaxpr/ppermute | solution.py:15
  30.5 7.9 %collective-permute-start.1 = (f32[2]{0:T(128)S(1)}, f32[2]{0:T(128)S(1)}, u32[]{:S(2)}, u32[]{:S(2)}) collective-permute-start(f32[2]{0:T(128)S(1)} %pad_maximum_fusion.2), channel_id=1, source_target_pairs={{0,8},{8,16},{16,24},{1,9},{9,17},{17,25},{2,10},{10,18},{18,26},{... | collective-permute-start | bytes 32 | tf_op jit(solution)/shard_map/while/body/eval_jaxpr/ppermute | solution.py:15
  40.4 14.7 %collective-permute-start = (f32[8,128,128]{2,1,0:T(8,128)S(1)}, f32[8,128,128]{2,1,0:T(8,128)S(1)}, u32[]{:S(2)}, u32[]{:S(2)}) collective-permute-start(f32[8,128,128]{2,1,0:T(8,128)S(1)} %select_add_fusion.2), channel_id=1, source_target_pairs={{0,8},{8,16},{16,24},{1,9},{9,17},{17,25},{2,10},{10,18},{18,26},{... | collective-permute-start | bytes 1572872 | tf_op jit(solution)/shard_map/while/body/eval_jaxpr/ppermute | solution.py:15
  48.2 6.9 %collective-permute-start.1 = (f32[2]{0:T(128)S(1)}, f32[2]{0:T(128)S(1)}, u32[]{:S(2)}, u32[]{:S(2)}) collective-permute-start(f32[2]{0:T(128)S(1)} %pad_maximum_fusion.2), channel_id=1, source_target_pairs={{0,8},{8,16},{16,24},{1,9},{9,17},{17,25},{2,10},{10,18},{18,26},{... | collective-permute-start | bytes 32 | tf_op jit(solution)/shard_map/while/body/eval_jaxpr/ppermute | solution.py:15
  57.2 13.7 %collective-permute-start = (f32[8,128,128]{2,1,0:T(8,128)S(1)}, f32[8,128,128]{2,1,0:T(8,128)S(1)}, u32[]{:S(2)}, u32[]{:S(2)}) collective-permute-start(f32[8,128,128]{2,1,0:T(8,128)S(1)} %select_add_fusion.2), channel_id=1, source_target_pairs={{0,8},{8,16},{16,24},{1,9},{9,17},{17,25},{2,10},{10,18},{18,26},{... | collective-permute-start | bytes 1572872 | tf_op jit(solution)/shard_map/while/body/eval_jaxpr/ppermute | solution.py:15
  64.9 5.9 %collective-permute-start.1 = (f32[2]{0:T(128)S(1)}, f32[2]{0:T(128)S(1)}, u32[]{:S(2)}, u32[]{:S(2)}) collective-permute-start(f32[2]{0:T(128)S(1)} %pad_maximum_fusion.2), channel_id=1, source_target_pairs={{0,8},{8,16},{16,24},{1,9},{9,17},{17,25},{2,10},{10,18},{18,26},{... | collective-permute-start | bytes 32 | tf_op jit(solution)/shard_map/while/body/eval_jaxpr/ppermute | solution.py:15
  74.2 3.1 copy-start.11
  82.4 1.6 copy-start.3
  93.0 1.6 copy-start.3
  103.6 1.6 copy-start.3
  103.6 1.6 copy-start.4
  122.5 2.4 copy-start.15
  123.3 1.7 copy-start.6
  128.9 4.9 %copy-start.14 = (bf16[1,768,1024]{1,2,0:T(8,128)(2,1)S(1)}, bf16[1,768,1024]{1,2,0:T(8,128)(2,1)}, u32[]{:S(2)}) copy-start(bf16[1,768,1024]{1,2,0:T(8,128)(2,1)} %copy.93) | copy-start | bytes 4718596
  192.2 3.7 %copy-start.7 = (f32[96,8,8,128]{3,2,1,0:T(8,128)S(1)}, f32[96,8,8,128]{3,2,1,0:T(8,128)}, u32[]{:S(2)}) copy-start(f32[96,8,8,128]{3,2,1,0:T(8,128)} %copy-done.6) | copy-start | bytes 9437188
  261.5 1.8 copy-start
  285.3 1.8 copy-start
  309.1 1.8 copy-start
  315.7 3.8 %copy-start.12 = (bf16[3,256,8,128]{3,2,1,0:T(8,128)(2,1)S(1)}, bf16[3,256,8,128]{3,2,1,0:T(8,128)(2,1)}, u32[]{:S(2)}) copy-start(bf16[3,256,8,128]{3,2,1,0:T(8,128)(2,1)} %get-tuple-element.545) | copy-start | bytes 4718596
  319.5 2.0 copy-start.13
  (10 other events, 13.9 us)
Sparse Core Ops, SparseCore 0:
  135.4 48.6 all-gather.3
where the time goes:
time: 334 us; the launch traced here: 330 us
  local copies, waits for them, and re-layouts  78.9 us (24%)
  blocking collectives  54.4 us (16%)
  matrix products  54.3 us (16%)
  loops' own time  48.1 us (14%)
  other arithmetic  40.1 us (12%)
  starting transfers between devices  24.2 us (7%)
  between operations  20 us (6%)
  waiting for transfers between devices  10.4 us (3%)
    psum x1, blocking collectives, body(): grad_gain = lax.psum(jnp.sum(cotangent * normed, axis=0), ('context', 'dp'))  39.9 us
    another operation x1, loops' own time, prefix(): return lax.fori_loop(0, size, step, start)  25.8 us
    ppermute x6, starting transfers between devices, shifted(): return lax.ppermute(block, axis, route)  24.2 us
    dynamic_slice x24, local copies, waits for them, and re-layouts, body(): lax.scan(forward_block, (state_in, first_seg), (block_q, block_k, block_v...  20.9 us
    another operation x1, loops' own time, body(): arrived = lax.fori_loop(0, lax.axis_size('context') - 1, relay_step, empty)  13.8 us
    all_gather x1, blocking collectives, prefix(): everything = jax.tree.map(lambda part: lax.all_gather(part, axis), value)  12 us
    unnamed x29, local copies, waits for them, and re-layouts  11.9 us
    ppermute x6, waiting for transfers between devices, shifted(): return lax.ppermute(block, axis, route)  10.4 us
  transfers between devices with their start and end apart: 7, of which 3 were waited for; matrix products, arithmetic and copies ran while one was open for 4% of the time, Pallas kernels for 0%

commit v1 on v0

--- a/solution.py
+++ b/solution.py
@@ -168,7 +168,9 @@
     radius = jnp.sqrt(squares / WIDTH + 1e-06)
     normed = attended / radius[:, None]
     normed_out = (normed * norm_gain).astype(jnp.bfloat16)
-    grad_gain = lax.psum(jnp.sum(cotangent * normed, axis=0), ("context", "dp"))
+    grad_gain = jnp.sum(cotangent * normed, axis=0)
+    for mesh_axis in ("dp", "context"):
+        grad_gain = lax.psum(grad_gain, mesh_axis)
     grad_att = (
         (gained - attended * (inner / (WIDTH * radius * radius))[:, None]) / radius[:, None]
     ).astype(jnp.bfloat16)

time: 334 us -> 317 us (0.949)
  blocking collectives: 54.4 us -> 33.9 us
  waiting for transfers between devices: 10.4 us -> 15.9 us
    psum x1 -> x2, blocking collectives: 39.9 us -> 19.4 us  [body(): grad_gain = lax.psum(grad_gain, mesh_axis)]
    all_gather x1, waiting for transfers between devices: 0.01 us -> 5.47 us  [prefix(): everything = jax.tree.map(lambda part: lax.all_gather(part, axis), value)]
  transfers between devices with their start and end apart: 7 -> 7, of which waited for: 3 -> 4; matrix products, arithmetic and copies ran while one was open for 4% -> 4% of each run, Pallas kernels for 0% -> 0%
where the time goes in v1:
time: 317 us; the launch traced here: 314 us
  local copies, waits for them, and re-layouts  78.8 us (25%)
  matrix products  54.3 us (17%)
  loops' own time  47 us (15%)
  other arithmetic  40.1 us (13%)
  blocking collectives  33.9 us (11%)
  starting transfers between devices  24.2 us (8%)
  between operations  19.9 us (6%)
  waiting for transfers between devices  15.9 us (5%)
    another operation x1, loops' own time, prefix(): return lax.fori_loop(0, size, step, start)  24.6 us
    ppermute x6, starting transfers between devices, shifted(): return lax.ppermute(block, axis, route)  24.2 us
    dynamic_slice x24, local copies, waits for them, and re-layouts, body(): lax.scan(forward_block, (state_in, first_seg), (block_q, block_k, block_v...  20.9 us
    psum x2, blocking collectives, body(): grad_gain = lax.psum(grad_gain, mesh_axis)  19.4 us
    another operation x1, loops' own time, body(): arrived = lax.fori_loop(0, lax.axis_size('context') - 1, relay_step, empty)  14 us
    all_gather x1, blocking collectives, prefix(): everything = jax.tree.map(lambda part: lax.all_gather(part, axis), value)  12 us
    unnamed x29, local copies, waits for them, and re-layouts  11.9 us
    ppermute x6, waiting for transfers between devices, shifted(): return lax.ppermute(block, axis, route)  10.4 us
  transfers between devices with their start and end apart: 7, of which 4 were waited for; matrix products, arithmetic and copies ran while one was open for 4% of the time, Pallas kernels for 0%

profile of v1, /device:TPU:0, one launch (start us, length us, event | category | flops | bytes accessed | tf_op | source)
XLA Modules:
  0.0 314.1 jit_solution(10235065618864790981)
XLA Ops:
  20.0 50.9 %while.71 = (s32[]{:T(128)}, f32[8,128,128]{2,1,0:T(8,128)S(1)}, f32[2]{0:T(128)S(1)}, f32[2]{0:T(128)S(1)}, pred[]{:T(512)}, /*index=5*/pred[]{:T(512)}, f32[8,...) while((s32[]{:T(128)}, f32[8,128,128]{2,1,0:T(8,128)S(1)}, f32[2]{0:T(128)S(1)}, f32[2]{0:T(128)S(1)}, ...), condition=%wide.region_1.2_spmd, body=%wide.region_0.1_spmd.sunk | while | flops 262154 | bytes 3670328 | solution.py:153
  22.2 5.0 %collective-permute-start = (f32[8,128,128]{2,1,0:T(8,128)S(1)}, f32[8,128,128]{2,1,0:T(8,128)S(1)}, u32[]{:S(2)}, u32[]{:S(2)}) collective-permute-start(f32[8,128,128]{2,1,0:T(8,128)S(1)} %select_add_fusion.2), channel_id=1, source_target_pairs={{0,8},{8,16},{16,24},{1,9},{9,17},{17,25},{2,10},{10,18},{18,26},{... | collective-permute-start | bytes 1572872 | tf_op jit(solution)/shard_map/while/body/eval_jaxpr/ppermute | solution.py:15
  30.5 3.4 %collective-permute-start.1 = (f32[2]{0:T(128)S(1)}, f32[2]{0:T(128)S(1)}, u32[]{:S(2)}, u32[]{:S(2)}) collective-permute-start(f32[2]{0:T(128)S(1)} %pad_maximum_fusion.2), channel_id=1, source_target_pairs={{0,8},{8,16},{16,24},{1,9},{9,17},{17,25},{2,10},{10,18},{18,26},{... | collective-permute-start | bytes 32 | tf_op jit(solution)/shard_map/while/body/eval_jaxpr/ppermute | solution.py:15
  33.9 4.4 %collective-permute-done.1 = f32[2]{0:T(128)S(1)} collective-permute-done((f32[2]{0:T(128)S(1)}, f32[2]{0:T(128)S(1)}, u32[]{:S(2)}, u32[]{:S(2)}) %collective-permute-start.1) | collective-permute-done | bytes 40 | tf_op jit(solution)/shard_map/while/body/eval_jaxpr/ppermute | solution.py:15
  40.5 4.4 %collective-permute-start = (f32[8,128,128]{2,1,0:T(8,128)S(1)}, f32[8,128,128]{2,1,0:T(8,128)S(1)}, u32[]{:S(2)}, u32[]{:S(2)}) collective-permute-start(f32[8,128,128]{2,1,0:T(8,128)S(1)} %select_add_fusion.2), channel_id=1, source_target_pairs={{0,8},{8,16},{16,24},{1,9},{9,17},{17,25},{2,10},{10,18},{18,26},{... | collective-permute-start | bytes 1572872 | tf_op jit(solution)/shard_map/while/body/eval_jaxpr/ppermute | solution.py:15
  48.2 3.4 %collective-permute-start.1 = (f32[2]{0:T(128)S(1)}, f32[2]{0:T(128)S(1)}, u32[]{:S(2)}, u32[]{:S(2)}) collective-permute-start(f32[2]{0:T(128)S(1)} %pad_maximum_fusion.2), channel_id=1, source_target_pairs={{0,8},{8,16},{16,24},{1,9},{9,17},{17,25},{2,10},{10,18},{18,26},{... | collective-permute-start | bytes 32 | tf_op jit(solution)/shard_map/while/body/eval_jaxpr/ppermute | solution.py:15
  51.7 3.5 %collective-permute-done.1 = f32[2]{0:T(128)S(1)} collective-permute-done((f32[2]{0:T(128)S(1)}, f32[2]{0:T(128)S(1)}, u32[]{:S(2)}, u32[]{:S(2)}) %collective-permute-start.1) | collective-permute-done | bytes 40 | tf_op jit(solution)/shard_map/while/body/eval_jaxpr/ppermute | solution.py:15
  57.3 4.4 %collective-permute-start = (f32[8,128,128]{2,1,0:T(8,128)S(1)}, f32[8,128,128]{2,1,0:T(8,128)S(1)}, u32[]{:S(2)}, u32[]{:S(2)}) collective-permute-start(f32[8,128,128]{2,1,0:T(8,128)S(1)} %select_add_fusion.2), channel_id=1, source_target_pairs={{0,8},{8,16},{16,24},{1,9},{9,17},{17,25},{2,10},{10,18},{18,26},{... | collective-permute-start | bytes 1572872 | tf_op jit(solution)/shard_map/while/body/eval_jaxpr/ppermute | solution.py:15
  65.0 3.4 %collective-permute-start.1 = (f32[2]{0:T(128)S(1)}, f32[2]{0:T(128)S(1)}, u32[]{:S(2)}, u32[]{:S(2)}) collective-permute-start(f32[2]{0:T(128)S(1)} %pad_maximum_fusion.2), channel_id=1, source_target_pairs={{0,8},{8,16},{16,24},{1,9},{9,17},{17,25},{2,10},{10,18},{18,26},{... | collective-permute-start | bytes 32 | tf_op jit(solution)/shard_map/while/body/eval_jaxpr/ppermute | solution.py:15
  74.3 3.1 copy.106
  80.5 32.1 %while.72 = (s32[]{:T(128)}, f32[8,128,128]{2,1,0:T(8,128)S(1)}, s32[]{:T(128)}, f32[3,256,8,128]{1,3,2,0:T(8,128)}, bf16[3,8,256,256]{3,2,1,0:T(8,128)(2,1)}, /...) while((s32[]{:T(128)}, f32[8,128,128]{2,1,0:T(8,128)S(1)}, ...), condition=%wide.region_3.4_spmd, body=%wide.region_2.3_spmd.sunk | while | flops 405209600 | bytes 18224672 | solution.py:158
  113.8 2.5 copy.70
  118.5 2.6 copy.93
  129.3 4.9 %fusion.54 = bf16[768,8,128]{2,1,0:T(8,128)(2,1)S(1)} fusion(f32[96,8,8,128]{3,2,1,0:T(8,128)} %copy-done.6, f32[3,256,8,128]{3,2,1,0:T(8,128)S(1)} %copy.70, f32[768]{0:T(1024)S(1)} %get-tuple-element.728, f32[768]{0:T(1024)S(1)} %get-tuple-element.727, f32[8,128]{1,0:T(8,128)S(1)} %bitcast.320), kind=kLoop, calls=%fused_computation.98 | loop fusion | flops 3932160 | bytes 7874560 | tf_op jit(solution)/shard_map/convert_element_type | solution.py:176
  135.7 12.0 %all-gather.1 = f32[4,1,2]{2,1,0:T(1,128)S(1)} all-gather(f32[1,1,2]{2,1,0:T(1,128)S(1)} %fusion.66), channel_id=1, replica_groups=mesh['context'=4,'tensor'=2,'dp'=4] {'context'}, dimensions={0}, use_global_device_ids=true | all-gather | bytes 40 | tf_op jit(solution)/shard_map/all_gather | solution.py:20
  152.6 9.9 %psum.30 = f32[1024]{0:T(1024)S(1)} all-reduce(f32[1024]{0:T(1024)S(1)} %fusion.51), channel_id=1, replica_groups=mesh['context'=4,'tensor'=2,'dp'=4] {'dp'}, use_global_device_ids=true, to_apply=%region_13.14 | all-reduce | flops 1024 | bytes 8192 | tf_op jit(solution)/shard_map/psum | solution.py:173
  162.5 9.5 %psum.31 = f32[1024]{0:T(1024)} all-reduce(f32[1024]{0:T(1024)S(1)} %psum.30), channel_id=1, replica_groups=mesh['context'=4,'tensor'=2,'dp'=4] {'context'}, use_global_device_ids=true, to_apply=%region_14.15 | all-reduce | flops 1024 | bytes 8192 | tf_op jit(solution)/shard_map/psum | solution.py:173
  172.0 3.7 %multiply_convert_fusion = bf16[1,768,1024]{2,1,0:T(8,128)(2,1)} fusion(f32[1,768,1024]{2,1,0:T(8,128)} %reshape.302, f32[1024]{0:T(1024)S(1)} %copy-done.15, f32[768]{0:T(1024)S(1)} %get-tuple-element.728), kind=kLoop, calls=%fused_computation.102 | loop fusion | flops 2359296 | bytes 4725760 | tf_op jit(solution)/shard_map/convert_element_type | solution.py:170
  175.7 2.9 divide_convert_fusion
  178.7 5.5 %all-gather.4.cloned.1.call-done = f32[32,128,128]{2,1,0:T(8,128)} async-done(((f32[8,128,128]{2,1,0:T(8,128)}), f32[32,128,128]{2,1,0:T(8,128)}) %all-gather.4.cloned.1.call-update) | async-done | bytes 2097168 | tf_op jit(solution)/shard_map/all_gather | solution.py:20
  184.2 38.2 %while.74 = (s32[]{:T(128)}, f32[8,128,128]{2,1,0:T(8,128)}, f32[2]{0:T(128)S(1)}, s32[]{:T(128)}, f32[4,8,128,128]{3,2,1,0:T(8,128)}, /*index=5*/f32[4,2]{0,1:T...) while((s32[]{:T(128)}, f32[8,128,128]{2,1,0:T(8,128)}, ...), condition=%wide.region_9.10_spmd.clone, body=%wide.region_8.9_spmd.clone.sunk | while | flops 524312 | bytes 1573215 | solution.py:33
  228.1 71.2 %while.73 = (s32[]{:T(128)}, f32[8,128,128]{2,1,0:T(8,128)S(1)}, bf16[3,256,8,128]{3,2,1,0:T(8,128)(2,1)}, bf16[3,256,8,128]{3,2,1,0:T(8,128)(2,1)}, bf16[3,256,...) while((s32[]{:T(128)}, f32[8,128,128]{2,1,0:T(8,128)S(1)}, ...), condition=%wide.region_11.12_spmd, body=%wide.region_10.11_spmd.sunk | while | flops 809697792 | bytes 39720800 | solution.py:188
  229.3 2.5 select_convert_fusion.3
  299.4 3.8 %reshape.304 = bf16[1,768,1024]{2,1,0:T(8,128)(2,1)} reshape(bf16[3,256,8,128]{3,2,1,0:T(8,128)(2,1)} %get-tuple-element.544) | data formatting | bytes 3145728 | tf_op jit(solution)/shard_map/reshape | solution.py:194
  (241 shorter events, 152.2 us)
Async XLA Ops:
  7.2 177.0 %all-gather.4.cloned.1.call-start = ((), (), s32[]{:S(2)}) async-start(), calls=%async_computation | async-start | bytes 2621440 | tf_op jit(solution)/shard_map/all_gather | solution.py:20
  14.3 2.0 copy-start.8
  16.3 1.7 copy-start.10
  20.0 53.3 %copy-start.16 = (s32[1,12]{1,0:T(1,128)S(1)}, s32[1,12]{1,0:T(1,128)}, u32[]{:S(2)}) copy-start(s32[1,12]{1,0:T(1,128)} %param.18) | copy-start | bytes 148
  22.2 16.1 %collective-permute-start = (f32[8,128,128]{2,1,0:T(8,128)S(1)}, f32[8,128,128]{2,1,0:T(8,128)S(1)}, u32[]{:S(2)}, u32[]{:S(2)}) collective-permute-start(f32[8,128,128]{2,1,0:T(8,128)S(1)} %select_add_fusion.2), channel_id=1, source_target_pairs={{0,8},{8,16},{16,24},{1,9},{9,17},{17,25},{2,10},{10,18},{18,26},{... | collective-permute-start | bytes 1572872 | tf_op jit(solution)/shard_map/while/body/eval_jaxpr/ppermute | solution.py:15
  30.5 7.9 %collective-permute-start.1 = (f32[2]{0:T(128)S(1)}, f32[2]{0:T(128)S(1)}, u32[]{:S(2)}, u32[]{:S(2)}) collective-permute-start(f32[2]{0:T(128)S(1)} %pad_maximum_fusion.2), channel_id=1, source_target_pairs={{0,8},{8,16},{16,24},{1,9},{9,17},{17,25},{2,10},{10,18},{18,26},{... | collective-permute-start | bytes 32 | tf_op jit(solution)/shard_map/while/body/eval_jaxpr/ppermute | solution.py:15
  40.5 14.7 %collective-permute-start = (f32[8,128,128]{2,1,0:T(8,128)S(1)}, f32[8,128,128]{2,1,0:T(8,128)S(1)}, u32[]{:S(2)}, u32[]{:S(2)}) collective-permute-start(f32[8,128,128]{2,1,0:T(8,128)S(1)} %select_add_fusion.2), channel_id=1, source_target_pairs={{0,8},{8,16},{16,24},{1,9},{9,17},{17,25},{2,10},{10,18},{18,26},{... | collective-permute-start | bytes 1572872 | tf_op jit(solution)/shard_map/while/body/eval_jaxpr/ppermute | solution.py:15
  48.2 6.9 %collective-permute-start.1 = (f32[2]{0:T(128)S(1)}, f32[2]{0:T(128)S(1)}, u32[]{:S(2)}, u32[]{:S(2)}) collective-permute-start(f32[2]{0:T(128)S(1)} %pad_maximum_fusion.2), channel_id=1, source_target_pairs={{0,8},{8,16},{16,24},{1,9},{9,17},{17,25},{2,10},{10,18},{18,26},{... | collective-permute-start | bytes 32 | tf_op jit(solution)/shard_map/while/body/eval_jaxpr/ppermute | solution.py:15
  57.3 13.7 %collective-permute-start = (f32[8,128,128]{2,1,0:T(8,128)S(1)}, f32[8,128,128]{2,1,0:T(8,128)S(1)}, u32[]{:S(2)}, u32[]{:S(2)}) collective-permute-start(f32[8,128,128]{2,1,0:T(8,128)S(1)} %select_add_fusion.2), channel_id=1, source_target_pairs={{0,8},{8,16},{16,24},{1,9},{9,17},{17,25},{2,10},{10,18},{18,26},{... | collective-permute-start | bytes 1572872 | tf_op jit(solution)/shard_map/while/body/eval_jaxpr/ppermute | solution.py:15
  65.0 5.9 %collective-permute-start.1 = (f32[2]{0:T(128)S(1)}, f32[2]{0:T(128)S(1)}, u32[]{:S(2)}, u32[]{:S(2)}) collective-permute-start(f32[2]{0:T(128)S(1)} %pad_maximum_fusion.2), channel_id=1, source_target_pairs={{0,8},{8,16},{16,24},{1,9},{9,17},{17,25},{2,10},{10,18},{18,26},{... | collective-permute-start | bytes 32 | tf_op jit(solution)/shard_map/while/body/eval_jaxpr/ppermute | solution.py:15
  74.3 3.1 copy-start.11
  82.5 1.6 copy-start.3
  82.5 1.6 copy-start.4
  103.9 1.6 copy-start.3
  103.9 1.6 copy-start.4
  122.9 2.4 copy-start.15
  123.7 1.6 copy-start.6
  129.3 4.9 %copy-start.14 = (bf16[1,768,1024]{1,2,0:T(8,128)(2,1)S(1)}, bf16[1,768,1024]{1,2,0:T(8,128)(2,1)}, u32[]{:S(2)}) copy-start(bf16[1,768,1024]{1,2,0:T(8,128)(2,1)} %copy.93) | copy-start | bytes 4718596
  172.0 3.7 %copy-start.7 = (f32[96,8,8,128]{3,2,1,0:T(8,128)S(1)}, f32[96,8,8,128]{3,2,1,0:T(8,128)}, u32[]{:S(2)}) copy-start(f32[96,8,8,128]{3,2,1,0:T(8,128)} %copy-done.6) | copy-start | bytes 9437188
  245.4 1.8 copy-start
  269.2 1.8 copy-start
  292.9 1.8 copy-start
  299.3 3.8 %copy-start.12 = (bf16[3,256,8,128]{3,2,1,0:T(8,128)(2,1)S(1)}, bf16[3,256,8,128]{3,2,1,0:T(8,128)(2,1)}, u32[]{:S(2)}) copy-start(bf16[3,256,8,128]{3,2,1,0:T(8,128)(2,1)} %get-tuple-element.545) | copy-start | bytes 4718596
  303.2 2.0 copy-start.13
  (10 other events, 13.9 us)
Sparse Core Ops, SparseCore 0:
  135.8 48.3 all-gather.3
